TPU v7x, 256 devices: a whole 4x4x8 slice. The times are simulated.
256 devices in a mesh: block: 16 (over z_hi, y), tok: 16 (over z_lo, x, core).
Axes of the slice: x: 4, y: 4, z: 8 (z_hi: 4, z_lo: 2; z = z_hi * 2 + z_lo), core: 2. Of those that a mesh axis runs over, the one named last changes fastest.
Arguments:
- queries: bfloat16 [262144, 512], P(('block', 'tok')), may hold values from -6 to 6
- keys: bfloat16 [262144, 512], P(('block', 'tok')), may hold values from -6 to 6
- values: bfloat16 [262144, 512], P(('block', 'tok')), may hold values from -6 to 6
- rates: float32 [3, 262144], P(None, ('block', 'tok')), may hold values from 0.3 to 3
- fast0: float32 [3, 512, 512], replicated, may hold values from -1 to 1
Outputs:
- outputs: bfloat16 [262144, 512], P(('block', 'tok'))
All inputs are finite; a program needn't handle non-finite values.
Results may differ from a plain program's by a relative error of at most 0.039.
Values may be sent and summed in bfloat16 or wider, within the bound.
No kernel may reach another device: no remote copies, remote signals or barrier semaphores. Data moves between devices by JAX's collectives and lax.ppermute only.
A program may use at most 128 MiB of HBM per device.

v0:
```python
import jax
import jax.numpy as jnp
from jax import lax
from jax.sharding import PartitionSpec as P


def carried_in(value, axis, join, neutral):
    place = lax.axis_index(axis)
    gathered = lax.all_gather(value.astype(jnp.bfloat16), axis)
    state = jnp.zeros_like(value) + jnp.asarray(neutral, value.dtype)

    def one(step, state):
        return join(state, lax.dynamic_index_in_dim(gathered, step, 0, False).astype(value.dtype))

    return lax.fori_loop(0, place, one, state)


def contract_cols(left, right):
    return lax.dot_general(
        left, right, (((1,), (1,)), ((), ())), preferred_element_type=jnp.float32
    )


def contract_rows(left, right):
    return lax.dot_general(
        left, right, (((0,), (0,)), ((), ())), preferred_element_type=jnp.float32
    )


def rescale(rows, target):
    return rows * (target / jnp.sqrt(jnp.sum(rows * rows, -1, keepdims=True) + 1e-06))


def fast_grads(weight_bf, keys, values, rates, scale):
    gate = contract_cols(keys, weight_bf[0])
    upper = contract_cols(keys, weight_bf[1])
    sigma = jax.nn.sigmoid(gate)
    active = gate * sigma
    hidden = active * upper
    back = -contract_cols(values, weight_bf[2])
    dgate = back * upper * sigma * (1.0 + gate * (1.0 - sigma))
    dupper = back * active
    rate = rates * scale
    grad_gate = contract_rows((rate[0][:, None] * dgate).astype(jnp.bfloat16), keys)
    grad_up = contract_rows((rate[1][:, None] * dupper).astype(jnp.bfloat16), keys)
    grad_down = -contract_rows((rate[2][:, None] * hidden).astype(jnp.bfloat16), values)
    return jnp.stack([grad_gate, grad_up, grad_down])


def apply_fast(weight_bf, queries):
    gate = contract_cols(queries, weight_bf[0])
    upper = contract_cols(queries, weight_bf[1])
    hidden = (jax.nn.silu(gate) * upper).astype(jnp.bfloat16)
    return jnp.dot(hidden, weight_bf[2], preferred_element_type=jnp.float32).astype(jnp.bfloat16)


def add_terms(earlier, later):
    return earlier + later


def shards(queries, keys, values, rates, fast0):
    groups = lax.axis_size("tok")
    scale = (keys.shape[0] * groups * keys.shape[1]) ** (-0.5)
    target = jnp.sqrt(jnp.sum(fast0 * fast0, -1, keepdims=True))
    weights = fast0
    for update_step in range(2):
        partial_grad = fast_grads(weights.astype(jnp.bfloat16), keys, values, rates, scale)
        total = lax.psum(partial_grad.astype(jnp.bfloat16), "tok").astype(jnp.float32)
        weights = rescale(weights - total, target)
    change = weights - fast0
    earlier = carried_in(change, "block", add_terms, jnp.zeros_like(change))
    applied = rescale(fast0 + (earlier + change), target).astype(jnp.bfloat16)
    return apply_fast(applied, queries)


def solution(mesh):
    return jax.shard_map(
        shards,
        mesh=mesh,
        in_specs=(
            P(("block", "tok"), None),
            P(("block", "tok"), None),
            P(("block", "tok"), None),
            P(None, ("block", "tok")),
            P(),
        ),
        out_specs=P(("block", "tok"), None),
        check_vma=False,
    )
```

profile of v0, /device:TPU:248, one launch (start us, length us, event | category | flops | bytes accessed | tf_op | source)
XLA Modules:
  0.0 626.2 jit_solution(16234509022687132216)
XLA Ops:
  6.5 2.2 convert_element_type.50
  8.7 0.7 fusion.38
  9.5 0.7 fusion.39
  10.3 0.4 copy-done.7
  10.7 0.7 fusion.40
  11.5 1.2 fusion.21
  12.7 1.4 fusion.20
  14.1 1.1 fusion.25
  15.3 1.3 pad_maximum_fusion
  16.6 0.0 all-reduce.5.cloned.1.call-start
  16.7 126.4 %all-reduce.3.cloned.1.call-done = bf16[3,512,512]{2,1,0:T(8,128)(2,1)} async-done(((bf16[3,512,512]{2,1,0:T(8,128)(2,1)}), bf16[3,512,512]{2,1,0:T(8,128)(2,1)}) %all-reduce.3.cloned.1.call-update) | async-done | bytes 1572880 | tf_op jit(solution)/shard_map/psum | solution.py:68
  143.0 3.2 multiply_reduce_fusion.3
  146.2 0.1 copy-done.2
  146.3 0.5 copy-done.4
  146.8 0.4 multiply_convert_fusion.1
  147.2 0.7 fusion.35
  147.9 0.7 fusion.36
  148.7 0.7 fusion.37
  149.4 1.1 fusion.24
  150.6 1.4 fusion.22
  152.0 1.2 fusion.23
  153.2 1.3 pad_maximum_fusion.1
  154.6 0.2 all-gather.3.cloned.1.call-start
  154.8 127.2 %all-reduce.5.cloned.1.call-done = bf16[3,512,512]{2,1,0:T(8,128)(2,1)} async-done(((bf16[3,512,512]{2,1,0:T(8,128)(2,1)}), bf16[3,512,512]{2,1,0:T(8,128)(2,1)}) %all-reduce.5.cloned.1.call-update) | async-done | bytes 1572880 | tf_op jit(solution)/shard_map/psum | solution.py:68
  282.1 3.0 multiply_reduce_fusion.1
  285.1 1.8 fusion
  286.9 288.4 %all-gather.3.cloned.1.call-done = bf16[48,512,512]{2,1,0:T(8,128)(2,1)} async-done(((bf16[3,512,512]{2,1,0:T(8,128)(2,1)}), bf16[48,512,512]{2,1,0:T(8,128)(2,1)}) %all-gather.3.cloned.1.call-update) | async-done | bytes 25165840 | tf_op jit(solution)/shard_map/all_gather | solution.py:9
  575.3 0.4 broadcast_in_dim.2
  575.7 33.1 %while.10 = (s32[]{:T(128)}, f32[3,512,512]{2,1,0:T(8,128)S(1)}, s32[]{:T(128)}, bf16[16,3,512,512]{3,2,1,0:T(8,128)(2,1)}, s32[]{:T(128)}, /*index=5*/s32[]{:T(128)}, s32[]{:T(128)}) while((s32[]{:T(128)}, f32[3,512,512]{2,1,0:T(8,128)S(1)}, s32[]{:T(128)}, bf16[16,3,512,512]{3,2,1,0:T(8,128)(2,1)}, s32[]{:T(128)}, /*index=5*/s32[]{:T(128)}, ...), condition=%wide.region_6.7_spmd, body=%wide.region_5.6_spmd.sunk | while | flops 1572869 | bytes 7864443 | solution.py:15
  575.7 2.2 convert_add_fusion.2
  577.9 2.2 convert_add_fusion.2
  580.1 2.2 convert_add_fusion.2
  582.3 2.2 convert_add_fusion.2
  584.6 2.2 convert_add_fusion.2
  586.8 2.2 convert_add_fusion.2
  589.0 2.2 convert_add_fusion.2
  591.2 2.2 convert_add_fusion.2
  593.4 2.2 convert_add_fusion.2
  595.6 2.2 convert_add_fusion.2
  597.8 2.2 convert_add_fusion.2
  600.0 2.2 convert_add_fusion.2
  602.2 2.2 convert_add_fusion.2
  604.4 2.2 convert_add_fusion.2
  606.7 2.2 convert_add_fusion.2
  608.9 3.6 multiply_reduce_fusion
  612.5 1.4 multiply_convert_fusion
  614.0 1.8 fusion.34
  615.8 3.9 convolution_convert_fusion
  (26 shorter events, 0.2 us)
Async XLA Ops:
  6.5 2.2 copy-start
  6.5 136.5 %all-reduce.3.cloned.1.call-start = ((), (), s32[]{:S(2)}) async-start(), calls=%async_computation | async-start | bytes 3145728 | tf_op jit(solution)/shard_map/psum | solution.py:68
  9.5 0.8 copy-start.9
  9.5 1.2 copy-start.7
  16.6 265.4 %all-reduce.5.cloned.1.call-start = ((), (), s32[]{:S(2)}) async-start(), calls=%async_computation.1 | async-start | bytes 3145728 | tf_op jit(solution)/shard_map/psum | solution.py:68
  143.0 3.3 copy-start.2
  143.0 3.8 copy-start.4
  153.2 128.8 %copy-start.3 = (f32[3,512,512]{2,1,0:T(8,128)S(1)}, f32[3,512,512]{2,1,0:T(8,128)}, u32[]{:S(2)}) copy-start(f32[3,512,512]{2,1,0:T(8,128)} %param.11) | copy-start | bytes 9437188
  154.6 420.7 %all-gather.3.cloned.1.call-start = ((), (), s32[]{:S(2)}) async-start(), calls=%async_computation.2 | async-start | bytes 26738688 | tf_op jit(solution)/shard_map/all_gather | solution.py:9
  282.1 3.0 copy-start.5
  282.1 3.0 copy-start.6
  612.5 1.4 copy-start.8
  615.7 3.9 copy-start.1
Sparse Core Ops, SparseCore 0:
  16.7 126.2 all-reduce.2
  154.7 127.2 all-reduce.4
  287.0 288.2 all-gather.2
where the time goes:
time: 627 us; the launch traced here: 626 us
  waiting for transfers between devices  542 us (86%)
  other arithmetic  51.1 us (8%)
  matrix products  17.7 us (3%)
  between operations  13.3 us (2%)
    all_gather x1, waiting for transfers between devices, carried_in(): gathered = lax.all_gather(value.astype(jnp.bfloat16), axis)  288 us
    psum x2, waiting for transfers between devices, shards(): lax.psum(partial_grad.astype(jnp.bfloat16), 'tok').astype(jnp.float32)  254 us
    add x15, other arithmetic, add_terms(): return earlier + later  32.7 us
  transfers between devices with their start and end apart: 3, of which 3 were waited for; matrix products, arithmetic and copies ran while one was open for 0% of the time, Pallas kernels for 0%

commit v1 on v0

--- a/solution.py
+++ b/solution.py
@@ -65,7 +65,9 @@
     weights = fast0
     for update_step in range(2):
         partial_grad = fast_grads(weights.astype(jnp.bfloat16), keys, values, rates, scale)
-        total = lax.psum(partial_grad.astype(jnp.bfloat16), "tok").astype(jnp.float32)
+        total = jnp.sum(lax.all_gather(partial_grad.astype(jnp.bfloat16), "tok"), axis=0).astype(
+            jnp.float32
+        )
         weights = rescale(weights - total, target)
     change = weights - fast0
     earlier = carried_in(change, "block", add_terms, jnp.zeros_like(change))

time: 627 us -> 668 us (1.065)
  other arithmetic: 51.1 us -> 77.6 us
  waiting for transfers between devices: 542 us -> 556 us
    all_gather x0 -> x2, waiting for transfers between devices: none -> 268 us  [shards(): lax.all_gather(partial_grad.astype(jnp.bfloat16), 'tok')]
    psum x2 -> x0, waiting for transfers between devices: 254 us -> none  [shards(): lax.psum(partial_grad.astype(jnp.bfloat16), 'tok').astype(jnp.float32)]
    reduce_sum x0 -> x2, other arithmetic: none -> 27.7 us  [shards(): jnp.sum(lax.all_gather(partial_grad.astype(jnp.bfloat16), 'tok'), axis=0)]
where the time goes in v1:
time: 668 us; the launch traced here: 667 us
  waiting for transfers between devices  556 us (83%)
  other arithmetic  77.6 us (12%)
  matrix products  16.7 us (2%)
  between operations  13.4 us (2%)
    all_gather x1, waiting for transfers between devices, carried_in(): gathered = lax.all_gather(value.astype(jnp.bfloat16), axis)  288 us
    all_gather x2, waiting for transfers between devices, shards(): lax.all_gather(partial_grad.astype(jnp.bfloat16), 'tok')  268 us
    add x15, other arithmetic, add_terms(): return earlier + later  32.7 us
    reduce_sum x2, other arithmetic, shards(): jnp.sum(lax.all_gather(partial_grad.astype(jnp.bfloat16), 'tok'), axis=0)  27.7 us
  transfers between devices with their start and end apart: 3, of which 3 were waited for; matrix products, arithmetic and copies ran while one was open for 0% of the time, Pallas kernels for 0%

profile of v1, /device:TPU:248, one launch (start us, length us, event | category | flops | bytes accessed | tf_op | source)
XLA Modules:
  0.0 667.1 jit_solution(7750291460850466948)
XLA Ops:
  6.5 2.2 convert_element_type.68
  8.7 0.7 fusion.38
  9.5 0.7 fusion.39
  10.3 0.4 copy-done.7
  10.7 0.7 fusion.40
  11.5 1.2 fusion.21
  12.7 1.4 fusion.20
  14.1 1.1 fusion.25
  15.3 1.4 pad_maximum_fusion
  16.7 133.8 %all-gather.5.cloned.1.call-done = bf16[16,3,512,512]{3,2,1,0:T(8,128)(2,1)} async-done(((bf16[1,3,512,512]{3,2,1,0:T(8,128)(2,1)}), bf16[16,3,512,512]{3,2,1,0:T(8,128)(2,1)}) %all-gather.5.cloned.1.call-update) | async-done | bytes 25165840 | tf_op jit(solution)/shard_map/all_gather | solution.py:68
  150.6 13.2 %reduce_sum.60 = bf16[3,512,512]{2,1,0:T(8,128)(2,1)S(1)} reduce(bf16[16,3,512,512]{3,2,1,0:T(8,128)(2,1)} %all-gather.5.cloned.1.call-done, bf16[]{:T(256)} %constant.27.clone.1), dimensions={0}, to_apply=%region_0.0 | reduce | flops 11796480 | bytes 26738690 | tf_op jit(solution)/shard_map/reduce_sum | solution.py:68
  163.8 3.2 multiply_reduce_fusion.3
  167.2 0.4 multiply_convert_fusion.1
  167.6 0.7 fusion.35
  168.3 0.7 fusion.36
  169.1 0.5 copy-done.8
  169.5 0.7 fusion.37
  170.3 1.2 fusion.24
  171.5 1.4 fusion.22
  172.9 1.2 fusion.23
  174.1 1.3 pad_maximum_fusion.1
  175.7 134.2 %all-gather.7.cloned.1.call-done = bf16[16,3,512,512]{3,2,1,0:T(8,128)(2,1)} async-done(((bf16[1,3,512,512]{3,2,1,0:T(8,128)(2,1)}), bf16[16,3,512,512]{3,2,1,0:T(8,128)(2,1)}) %all-gather.7.cloned.1.call-update) | async-done | bytes 25165840 | tf_op jit(solution)/shard_map/all_gather | solution.py:68
  310.0 14.5 %reduce_sum.63 = bf16[3,512,512]{2,1,0:T(8,128)(2,1)} reduce(bf16[16,3,512,512]{3,2,1,0:T(8,128)(2,1)} %all-gather.7.cloned.1.call-done, bf16[]{:T(256)} %constant.27.clone.1), dimensions={0}, to_apply=%region_3.0 | reduce | flops 11796480 | bytes 26738690 | tf_op jit(solution)/shard_map/reduce_sum | solution.py:68
  324.4 3.0 multiply_reduce_fusion.1
  327.5 1.8 fusion
  329.3 287.9 %all-gather.9.cloned.1.call-done = bf16[48,512,512]{2,1,0:T(8,128)(2,1)} async-done(((bf16[3,512,512]{2,1,0:T(8,128)(2,1)}), bf16[48,512,512]{2,1,0:T(8,128)(2,1)}) %all-gather.9.cloned.1.call-update) | async-done | bytes 25165840 | tf_op jit(solution)/shard_map/all_gather | solution.py:9
  617.2 0.4 broadcast_in_dim.2
  617.6 33.1 %while.10 = (s32[]{:T(128)}, f32[3,512,512]{2,1,0:T(8,128)S(1)}, s32[]{:T(128)}, bf16[16,3,512,512]{3,2,1,0:T(8,128)(2,1)}, s32[]{:T(128)}, /*index=5*/s32[]{:T(128)}, s32[]{:T(128)}) while((s32[]{:T(128)}, f32[3,512,512]{2,1,0:T(8,128)S(1)}, s32[]{:T(128)}, bf16[16,3,512,512]{3,2,1,0:T(8,128)(2,1)}, s32[]{:T(128)}, /*index=5*/s32[]{:T(128)}, ...), condition=%wide.region_6.7_spmd, body=%wide.region_5.6_spmd.sunk | while | flops 1572869 | bytes 7864443 | solution.py:15
  617.6 2.2 convert_add_fusion.2
  619.8 2.2 convert_add_fusion.2
  622.0 2.2 convert_add_fusion.2
  624.2 2.2 convert_add_fusion.2
  626.4 2.2 convert_add_fusion.2
  628.6 2.2 convert_add_fusion.2
  630.9 2.2 convert_add_fusion.2
  633.1 2.2 convert_add_fusion.2
  635.3 2.2 convert_add_fusion.2
  637.5 2.2 convert_add_fusion.2
  639.7 2.2 convert_add_fusion.2
  641.9 2.2 convert_add_fusion.2
  644.1 2.2 convert_add_fusion.2
  646.3 2.2 convert_add_fusion.2
  648.5 2.2 convert_add_fusion.2
  650.7 3.6 multiply_reduce_fusion
  654.4 0.3 multiply_convert_fusion
  654.7 1.1 copy-done.9
  655.8 0.7 fusion.34
  656.6 3.9 convolution_convert_fusion
  (32 shorter events, 0.6 us)
Async XLA Ops:
  6.5 2.2 copy-start
  6.5 144.0 %all-gather.5.cloned.1.call-start = ((), (), s32[]{:S(2)}) async-start(), calls=%async_computation | async-start | bytes 26738688 | tf_op jit(solution)/shard_map/all_gather | solution.py:68
  9.5 0.8 copy-start.11
  9.5 1.2 copy-start.7
  16.7 293.3 %all-gather.7.cloned.1.call-start = ((), (), s32[]{:S(2)}) async-start(), calls=%async_computation.1 | async-start | bytes 26738688 | tf_op jit(solution)/shard_map/all_gather | solution.py:68
  163.7 4.6 copy-start.4
  163.8 3.4 copy-start.2
  168.3 1.2 copy-start.8
  175.5 441.7 %all-gather.9.cloned.1.call-start = ((), (), s32[]{:S(2)}) async-start(), calls=%async_computation.2 | async-start | bytes 26738688 | tf_op jit(solution)/shard_map/all_gather | solution.py:9
  310.0 14.5 %copy-start.3 = (f32[3,512,512]{2,1,0:T(8,128)S(1)}, f32[3,512,512]{2,1,0:T(8,128)}, u32[]{:S(2)}) copy-start(f32[3,512,512]{2,1,0:T(8,128)} %param.11) | copy-start | bytes 9437188
  324.4 3.0 copy-start.5
  324.4 3.0 copy-start.6
  654.4 1.4 copy-start.10
  654.7 1.1 copy-start.9
  656.6 4.0 copy-start.1
Sparse Core Ops, SparseCore 0:
  16.8 133.7 all-gather.4
  175.6 134.3 all-gather.6
  329.4 287.7 all-gather.8
